TPU v7x, 512 devices: a whole 4x8x8 slice. The times are simulated.
512 devices in a mesh: vocab: 64 (over y, x, core), width: 8 (over z).
Axes of the slice: x: 4, y: 8, z: 8, core: 2. Of those that a mesh axis runs over, the one named last changes fastest.
Arguments:
- hidden: bfloat16 [8192, 2048], P('vocab', 'width'), may hold values from -400 to 400
- norm_gain: bfloat16 [2048], P('width'), may hold values from 0.5 to 1.5
- head_weight: bfloat16 [102400, 2048], P('vocab', 'width'), may hold values from -1 to 1
- targets: int32 [8192], P(('vocab', 'width')), may hold values from 0 to 102399
- pad_mask: int32 [8192], P(('vocab', 'width')), may hold values 0 or 1
- lengths: int32 [64], replicated, may hold values from 1 to 2048, 8192 in all
Outputs:
- entropy: float32 [8192], P(('vocab', 'width'))
- token_logprob: float32 [8192], P(('vocab', 'width'))
- seq_score: float32 [64], replicated
Inputs may be any that keep to these rules, and one draw needn't show every extreme that they name: The lengths sum to 8192.
All inputs are finite; a program needn't handle non-finite values. No bound on the sum of `pad_mask` on one device may be relied on, other than what follows from the above.
Results may differ from a plain program's by a relative error of at most 0.0031.
Values may be sent and summed in bfloat16 or wider, within the bound.
A program may use at most 64 MiB of HBM per device.

v0:
```python
import math
import jax
import jax.numpy as jnp
from jax import lax
from jax.sharding import PartitionSpec as P

epsilon = 1e-06


def merged_2(value, axis, join):
    pieces = jax.tree.map(lambda part: lax.all_gather(part, axis), value)
    head = jax.tree.map(lambda part: part[0], pieces)
    tail = jax.tree.map(lambda part: part[1:], pieces)
    total, _ = lax.scan(lambda total, piece: (join(total, piece), None), head, tail)
    return total


def summarize(logits, block_ids, first_col):
    peak = jnp.max(logits, axis=1)
    shifted = logits - peak[:, None]
    weights = jnp.exp(shifted)
    exp_total = jnp.sum(weights, axis=1)
    spread = jnp.sum(weights * shifted, axis=1)
    columns = first_col + lax.iota(jnp.int32, logits.shape[1])
    target_logit = jnp.sum(jnp.where(columns[None, :] == block_ids[:, None], logits, 0.0), axis=1)
    return (peak, exp_total, spread, target_logit)


def combine(earlier, later):
    peak = jnp.maximum(earlier[0], later[0])
    left_lift = jnp.exp(earlier[0] - peak)
    right_lift = jnp.exp(later[0] - peak)
    exp_total = earlier[1] * left_lift + later[1] * right_lift
    spread = left_lift * (earlier[2] + (earlier[0] - peak) * earlier[1]) + right_lift * (
        later[2] + (later[0] - peak) * later[1]
    )
    return (peak, exp_total, spread, earlier[3] + later[3])


def per_device(hidden, norm_gain, head_weight, targets, pad_mask, lengths):
    width_count = lax.axis_size("width")
    own_count = targets.shape[0]
    values = hidden.astype(jnp.float32)
    energy = lax.psum(jnp.sum(values * values, axis=1), "width")
    inv_rms = lax.rsqrt(energy / (hidden.shape[1] * width_count) + epsilon)
    normed = (values * inv_rms[:, None] * norm_gain.astype(jnp.float32)[None, :]).astype(
        jnp.bfloat16
    )
    full_rows = lax.all_to_all(normed, "width", split_axis=0, concat_axis=1, tiled=True)
    gathered, gathered_ids = (
        lax.all_gather(full_rows, "vocab", axis=0, tiled=True),
        lax.all_gather(targets, "vocab", axis=0, tiled=True),
    )
    col_count = head_weight.shape[0]
    first_col = lax.axis_index("vocab") * col_count
    total_rows = gathered.shape[0]
    block_rows = math.gcd(total_rows, 512)
    contract = (((1,), (1,)), ((), ()))
    head_full = lax.all_gather(head_weight, "width", axis=1, tiled=True)

    def per_block(inputs):
        logits = lax.dot_general(inputs[0], head_full, contract, preferred_element_type=jnp.float32)
        return summarize(logits, inputs[1], first_col)

    blocked = lax.map(
        per_block,
        (gathered.reshape(-1, block_rows, gathered.shape[1]), gathered_ids.reshape(-1, block_rows)),
    )
    statistics = (
        blocked[0].reshape(-1),
        blocked[1].reshape(-1),
        blocked[2].reshape(-1),
        blocked[3].reshape(-1),
    )
    merged = merged_2(statistics, "vocab", combine)
    own_start = lax.axis_index("vocab") * own_count
    peak = lax.dynamic_slice_in_dim(merged[0], own_start, own_count, 0)
    exp_total = lax.dynamic_slice_in_dim(merged[1], own_start, own_count, 0)
    spread = lax.dynamic_slice_in_dim(merged[2], own_start, own_count, 0)
    target_logit = lax.dynamic_slice_in_dim(merged[3], own_start, own_count, 0)
    kept_mask = pad_mask.astype(jnp.float32)
    log_total = jnp.log(exp_total)
    entropy = kept_mask * (log_total - spread / exp_total)
    token_logprob = kept_mask * (target_logit - peak - log_total)
    device_index = lax.axis_index("vocab") * width_count + lax.axis_index("width")
    token_index = device_index * own_count + lax.iota(jnp.int32, own_count)
    seq_ends = jnp.cumsum(lengths)
    seq_starts = seq_ends - lengths
    member = (
        (token_index[:, None] >= seq_starts[None, :]) & (token_index[:, None] < seq_ends[None, :])
    ).astype(jnp.float32)
    partial_value = jnp.sum(member * token_logprob[:, None], axis=0)
    seq_score = lax.psum(partial_value, ("vocab", "width")) / lengths.astype(jnp.float32)
    return (entropy, token_logprob, seq_score)


def solution(mesh):
    placed = (
        P("vocab", "width"),
        P("width"),
        P("vocab", "width"),
        P(("vocab", "width")),
        P(("vocab", "width")),
        P(),
    )
    return jax.shard_map(
        per_device,
        mesh=mesh,
        in_specs=placed,
        out_specs=(P(("vocab", "width")), P(("vocab", "width")), P()),
        check_vma=False,
    )
```

profile of v0, /device:TPU:1, one launch (start us, length us, event | category | flops | bytes accessed | tf_op | source)
XLA Modules:
  0.0 491.1 jit_solution(4575408305845917003)
XLA Ops:
  7.2 0.9 fusion.5
  8.2 20.3 %psum.14 = f32[128]{0:T(128)S(1)} all-reduce(f32[128]{0:T(128)S(1)} %fusion.5), channel_id=1, replica_groups=mesh['vocab'=64,'width'=8] {'width'}, use_global_device_ids=true, to_apply=%region_1.0 | all-reduce | flops 128 | bytes 1024 | tf_op jit(solution)/shard_map/psum | solution.py:44
  28.4 0.7 convert_element_type.18
  29.1 0.9 fusion.7
  30.0 9.6 %all_to_all.19 = bf16[8,16,256]{2,1,0:T(8,128)(2,1)S(1)} all-to-all(bf16[8,16,256]{2,1,0:T(8,128)(2,1)S(1)} %bitcast.73), channel_id=1, replica_groups=mesh['vocab'=64,'width'=8] {'width'}, dimensions={0} | all-to-all | bytes 131072 | tf_op jit(solution)/shard_map/all_to_all | solution.py:49
  40.3 0.7 all-gather.9.cloned.1.call-update
  41.1 1.3 dynamic-slice
  43.0 0.9 dynamic-update-slice
  43.9 22.5 %all-reduce = s32[1024]{0:T(1024)S(1)} all-reduce(s32[1024]{0:T(1024)S(1)} %dynamic-update-slice), channel_id=1, replica_groups=mesh['vocab'=64,'width'=8] {'vocab'}, use_global_device_ids=true, to_apply=%add | all-reduce | flops 1024 | bytes 8192
  66.4 0.7 copy.16
  67.4 0.7 sub.31
  68.0 58.4 %all-gather.7.cloned.1.call-done = bf16[1024,2048]{1,0:T(8,128)(2,1)} async-done(((bf16[16,2048]{1,0:T(8,128)(2,1)}), bf16[1024,2048]{1,0:T(8,128)(2,1)}) %all-gather.7.cloned.1.call-update) | async-done | bytes 4194320 | tf_op jit(solution)/shard_map/all_gather | solution.py:51
  126.4 83.2 %all-gather.9.cloned.1.call-done = bf16[1600,2048]{1,0:T(8,128)(2,1)} async-done(((bf16[1600,256]{1,0:T(8,128)(2,1)}), bf16[1600,2048]{1,0:T(8,128)(2,1)}) %all-gather.9.cloned.1.call-update) | async-done | bytes 6553616 | tf_op jit(solution)/shard_map/all_gather | solution.py:59
  209.6 16.2 %while.32 = (s32[]{:T(128)}, f32[2,512]{1,0:T(2,128)S(1)}, f32[2,512]{1,0:T(2,128)S(1)}, f32[2,512]{1,0:T(2,128)S(1)}, f32[2,512]{1,0:T(2,128)S(1)}, /*index=5*/...) while((s32[]{:T(128)}, f32[2,512]{1,0:T(2,128)S(1)}, ...), condition=%wide.region_7.8_spmd, body=%wide.region_2.7_spmd.sunk | while | flops 3361996288 | bytes 15250565 | solution.py:65
  209.6 6.4 %fusion.14 = (f32[512]{0:T(512)S(1)}, f32[512,1600]{0,1:T(8,128)S(1)}) fusion(bf16[1600,2048]{1,0:T(8,128)(2,1)} %get-tuple-element.320, bf16[2,512,2048]{2,1,0:T(8,128)(2,1)} %get-tuple-element.319, s32[]{:T(128)} %get-tuple-element.303), kind=kOutput, calls=%fused_computation.31.clone.1 | convolution fusion | flops 3356261888 | bytes 11930112 | tf_op jit(solution)/shard_map/while/body/eval_jaxpr/dot_general | solution.py:62
  216.1 1.4 fusion.15
  217.7 6.4 %fusion.14 = (f32[512]{0:T(512)S(1)}, f32[512,1600]{0,1:T(8,128)S(1)}) fusion(bf16[1600,2048]{1,0:T(8,128)(2,1)} %get-tuple-element.320, bf16[2,512,2048]{2,1,0:T(8,128)(2,1)} %get-tuple-element.319, s32[]{:T(128)} %get-tuple-element.303), kind=kOutput, calls=%fused_computation.31.clone.1 | convolution fusion | flops 3356261888 | bytes 11930112 | tf_op jit(solution)/shard_map/while/body/eval_jaxpr/dot_general | solution.py:62
  224.2 1.4 fusion.15
  225.8 42.7 %all-gather = f32[64,1,1024]{2,1,0:T(1,128)S(1)} all-gather(f32[1,1,1024]{2,1,0:T(1,128)S(1)} %reshape.60), channel_id=1, replica_groups=mesh['vocab'=64,'width'=8] {'vocab'}, dimensions={0}, use_global_device_ids=true | all-gather | bytes 266240 | tf_op jit(solution)/shard_map/all_gather | solution.py:11
  268.6 37.2 %all-gather.1 = f32[64,1,1024]{2,1,0:T(1,128)S(1)} all-gather(f32[1,1,1024]{2,1,0:T(1,128)S(1)} %reshape.62), channel_id=1, replica_groups=mesh['vocab'=64,'width'=8] {'vocab'}, dimensions={0}, use_global_device_ids=true | all-gather | bytes 266240 | tf_op jit(solution)/shard_map/all_gather | solution.py:11
  305.8 36.9 %all-gather.2 = f32[64,1,1024]{2,1,0:T(1,128)S(1)} all-gather(f32[1,1,1024]{2,1,0:T(1,128)S(1)} %reshape.64), channel_id=1, replica_groups=mesh['vocab'=64,'width'=8] {'vocab'}, dimensions={0}, use_global_device_ids=true | all-gather | bytes 266240 | tf_op jit(solution)/shard_map/all_gather | solution.py:11
  342.7 37.1 %all-gather.3 = f32[64,1,1024]{2,1,0:T(1,128)S(1)} all-gather(f32[1,1,1024]{2,1,0:T(1,128)S(1)} %reshape.66), channel_id=1, replica_groups=mesh['vocab'=64,'width'=8] {'vocab'}, dimensions={0}, use_global_device_ids=true | all-gather | bytes 266240 | tf_op jit(solution)/shard_map/all_gather | solution.py:11
  380.2 7.6 %while.33 = (s32[]{:T(128)}, f32[1024]{0:T(1024)S(1)}, f32[1024]{0:T(1024)S(1)}, f32[1024]{0:T(1024)S(1)}, f32[1024]{0:T(1024)S(1)}, /*index=5*/f32[63,1024]{1,0...) while((s32[]{:T(128)}, f32[1024]{0:T(1024)S(1)}, ...), condition=%wide.region_9.10_spmd, body=%wide.region_8.9_spmd.sunk | while | flops 16386 | bytes 110701 | solution.py:14
  388.4 95.3 %psum.15 = f32[64]{0:T(128)S(1)} all-reduce(f32[64]{0:T(128)S(1)} %select_reduce_fusion.1), channel_id=1, replica_groups=mesh['vocab'=64,'width'=8] {'vocab','width'}, use_global_device_ids=true, to_apply=%region_12.13 | all-reduce | flops 64 | bytes 512 | tf_op jit(solution)/shard_map/psum | solution.py:93
  (429 shorter events, 6.7 us)
Async XLA Ops:
  7.2 119.3 %all-gather.7.cloned.1.call-start = ((), (), s32[]{:S(2)}) async-start(), calls=%async_computation.1 | async-start | bytes 4259840 | tf_op jit(solution)/shard_map/all_gather | solution.py:51
  40.3 169.3 %all-gather.9.cloned.1.call-start = ((), (), s32[]{:S(2)}) async-start(), calls=%async_computation.2 | async-start | bytes 7372800 | tf_op jit(solution)/shard_map/all_gather | solution.py:59
  225.8 162.0 %copy-start.2 = (s32[16]{0:T(128)S(1)}, s32[16]{0:T(128)}, u32[]{:S(2)}) copy-start(s32[16]{0:T(128)} %param.14) | copy-start | bytes 196
  225.8 257.9 %copy-start.1 = (s32[64]{0:T(128)S(1)}, s32[64]{0:T(128)}, u32[]{:S(2)}) copy-start(s32[64]{0:T(128)} %param.15) | copy-start | bytes 772
  388.3 95.9 %copy-start = (f32[16]{0:T(128)}, f32[16]{0:T(128)S(1)}, u32[]{:S(2)}) copy-start(f32[16]{0:T(128)S(1)} %get-tuple-element.158) | copy-start | bytes 196
Sparse Core Ops, SparseCore 0:
  40.4 85.9 all-gather.6
  128.4 81.1 all-gather.8
where the time goes:
time: 491 us
  blocking collectives  302 us (62%)
  waiting for transfers between devices  142 us (29%)
  between operations  14.9 us (3%)
  matrix products  12.9 us (3%)
  other arithmetic  9.19 us (2%)
  local copies, waits for them, and re-layouts  6.36 us (1%)
    all_gather x4, blocking collectives, merged_2(): pieces = jax.tree.map(lambda part: lax.all_gather(part, axis), value)  154 us
    psum x1, blocking collectives, per_device(): lax.psum(partial_value, ('vocab', 'width')) / lengths.astype(jnp.float32)  95.3 us
    all_gather x1, waiting for transfers between devices, per_device(): head_full = lax.all_gather(head_weight, 'width', axis=1, tiled=True)  83.2 us
    all_gather x1, waiting for transfers between devices, per_device(): lax.all_gather(full_rows, 'vocab', axis=0, tiled=True)  58.4 us
    unnamed x1, blocking collectives  22.5 us
    psum x1, blocking collectives, per_device(): energy = lax.psum(jnp.sum(values * values, axis=1), 'width')  20.3 us
    dot_general x2, matrix products, per_block(): lax.dot_general(inputs[0], head_full, contract, preferred_element_type=jn...  12.9 us
  transfers between devices with their start and end apart: 2, of which 2 were waited for; matrix products, arithmetic and copies ran while one was open for 1% of the time, Pallas kernels for 0%

commit v1 on v0

--- a/solution.py
+++ b/solution.py
@@ -48,7 +48,9 @@
     )
     full_rows = lax.all_to_all(normed, "width", split_axis=0, concat_axis=1, tiled=True)
     gathered, gathered_ids = (
-        lax.all_gather(full_rows, "vocab", axis=0, tiled=True),
+        jnp.concatenate(
+            lax.all_to_all(jnp.stack([full_rows] * lax.axis_size("vocab")), "vocab", 0, 0), axis=0
+        ),
         lax.all_gather(targets, "vocab", axis=0, tiled=True),
     )
     col_count = head_weight.shape[0]

time: 491 us -> 437 us (0.89)
  waiting for transfers between devices: 142 us -> 0.7 us
  blocking collectives: 302 us -> 373 us
  starting transfers between devices: 0.08 us -> 16 us
    all_gather x1, waiting for transfers between devices: 83.2 us -> 0.02 us  [per_device(): head_full = lax.all_gather(head_weight, 'width', axis=1, tiled=True)]
    unnamed x1, blocking collectives: 22.5 us -> 96.5 us
    all_gather x1 -> x0, waiting for transfers between devices: 58.4 us -> none  [per_device(): lax.all_gather(full_rows, 'vocab', axis=0, tiled=True)]
    all_to_all x0 -> x1, starting transfers between devices: none -> 16 us  [per_device(): lax.all_to_all(jnp.stack([full_rows] * lax.axis_size('vocab')), 'vocab',...]
  transfers between devices with their start and end apart: 2 -> 2, of which waited for: 2 -> 0; matrix products, arithmetic and copies ran while one was open for 1% -> 2% of each run, Pallas kernels for 0% -> 0%
where the time goes in v1:
time: 437 us
  blocking collectives  373 us (85%)
  starting transfers between devices  16 us (4%)
  between operations  14.9 us (3%)
  matrix products  12.9 us (3%)
  other arithmetic  8.54 us (2%)
  local copies, waits for them, and re-layouts  7.05 us (2%)
    all_gather x4, blocking collectives, merged_2(): pieces = jax.tree.map(lambda part: lax.all_gather(part, axis), value)  151 us
    unnamed x1, blocking collectives  96.5 us
    psum x1, blocking collectives, per_device(): lax.psum(partial_value, ('vocab', 'width')) / lengths.astype(jnp.float32)  94.6 us
    psum x1, blocking collectives, per_device(): energy = lax.psum(jnp.sum(values * values, axis=1), 'width')  20.3 us
    all_to_all x1, starting transfers between devices, per_device(): lax.all_to_all(jnp.stack([full_rows] * lax.axis_size('vocab')), 'vocab',...  16 us
    dot_general x2, matrix products, per_block(): lax.dot_general(inputs[0], head_full, contract, preferred_element_type=jn...  12.9 us
    all_to_all x1, blocking collectives, per_device(): lax.all_to_all(normed, 'width', split_axis=0, concat_axis=1, tiled=True)  10.3 us
  transfers between devices with their start and end apart: 2, of which 0 were waited for; matrix products, arithmetic and copies ran while one was open for 2% of the time, Pallas kernels for 0%

profile of v1, /device:TPU:1, one launch (start us, length us, event | category | flops | bytes accessed | tf_op | source)
XLA Modules:
  0.0 436.7 jit_solution(9345876188455136609)
XLA Ops:
  7.2 0.7 all-gather.6.cloned.1.call-update
  7.9 0.7 convert_element_type.18
  8.6 0.9 fusion.5
  9.5 20.3 %psum.14 = f32[128]{0:T(128)S(1)} all-reduce(f32[128]{0:T(128)S(1)} %fusion.5), channel_id=1, replica_groups=mesh['vocab'=64,'width'=8] {'width'}, use_global_device_ids=true, to_apply=%region_1.0 | all-reduce | flops 128 | bytes 1024 | tf_op jit(solution)/shard_map/psum | solution.py:44
  29.8 0.9 fusion.7
  30.7 10.3 %all_to_all.21 = bf16[8,16,256]{2,1,0:T(8,128)(2,1)S(1)} all-to-all(bf16[8,16,256]{2,1,0:T(8,128)(2,1)S(1)} %bitcast.73), channel_id=1, replica_groups=mesh['vocab'=64,'width'=8] {'width'}, dimensions={0} | all-to-all | bytes 131072 | tf_op jit(solution)/shard_map/all_to_all | solution.py:49
  41.0 2.6 stack.5
  43.6 16.0 %all-to-all-start.1 = ((bf16[64,16,2048]{2,1,0:T(8,128)(2,1)}), bf16[64,16,2048]{2,1,0:T(8,128)(2,1)}, u32[]{:S(2)}, u32[]{:S(2)}) async-start(bf16[64,16,2048]{2,1,0:T(8,128)(2,1)} %stack.5), calls=%async_computation.1 | async-start | bytes 8388608 | tf_op jit(solution)/shard_map/all_to_all | solution.py:52
  59.6 1.3 dynamic-slice
  61.5 0.2 dynamic-update-slice
  61.8 96.5 %all-reduce = s32[1024]{0:T(1024)S(1)} all-reduce(s32[1024]{0:T(1024)S(1)} %dynamic-update-slice), channel_id=1, replica_groups=mesh['vocab'=64,'width'=8] {'vocab'}, use_global_device_ids=true, to_apply=%add | all-reduce | flops 1024 | bytes 8192
  158.6 16.2 %while.32 = (s32[]{:T(128)}, f32[2,512]{1,0:T(2,128)S(1)}, f32[2,512]{1,0:T(2,128)S(1)}, f32[2,512]{1,0:T(2,128)S(1)}, f32[2,512]{1,0:T(2,128)S(1)}, /*index=5*/...) while((s32[]{:T(128)}, f32[2,512]{1,0:T(2,128)S(1)}, ...), condition=%wide.region_7.8_spmd, body=%wide.region_2.7_spmd.sunk | while | flops 3361996288 | bytes 15250565 | solution.py:67
  158.6 6.4 %fusion.14 = (f32[512]{0:T(512)S(1)}, f32[512,1600]{0,1:T(8,128)S(1)}) fusion(bf16[1600,2048]{1,0:T(8,128)(2,1)} %get-tuple-element.320, bf16[2,512,2048]{2,1,0:T(8,128)(2,1)} %get-tuple-element.319, s32[]{:T(128)} %get-tuple-element.303), kind=kOutput, calls=%fused_computation.31.clone.1 | convolution fusion | flops 3356261888 | bytes 11930112 | tf_op jit(solution)/shard_map/while/body/eval_jaxpr/dot_general | solution.py:64
  165.1 1.4 fusion.15
  166.7 6.4 %fusion.14 = (f32[512]{0:T(512)S(1)}, f32[512,1600]{0,1:T(8,128)S(1)}) fusion(bf16[1600,2048]{1,0:T(8,128)(2,1)} %get-tuple-element.320, bf16[2,512,2048]{2,1,0:T(8,128)(2,1)} %get-tuple-element.319, s32[]{:T(128)} %get-tuple-element.303), kind=kOutput, calls=%fused_computation.31.clone.1 | convolution fusion | flops 3356261888 | bytes 11930112 | tf_op jit(solution)/shard_map/while/body/eval_jaxpr/dot_general | solution.py:64
  173.2 1.4 fusion.15
  174.9 40.3 %all-gather = f32[64,1,1024]{2,1,0:T(1,128)S(1)} all-gather(f32[1,1,1024]{2,1,0:T(1,128)S(1)} %reshape.59), channel_id=1, replica_groups=mesh['vocab'=64,'width'=8] {'vocab'}, dimensions={0}, use_global_device_ids=true | all-gather | bytes 266240 | tf_op jit(solution)/shard_map/all_gather | solution.py:11
  215.2 36.9 %all-gather.1 = f32[64,1,1024]{2,1,0:T(1,128)S(1)} all-gather(f32[1,1,1024]{2,1,0:T(1,128)S(1)} %reshape.61), channel_id=1, replica_groups=mesh['vocab'=64,'width'=8] {'vocab'}, dimensions={0}, use_global_device_ids=true | all-gather | bytes 266240 | tf_op jit(solution)/shard_map/all_gather | solution.py:11
  252.1 37.2 %all-gather.2 = f32[64,1,1024]{2,1,0:T(1,128)S(1)} all-gather(f32[1,1,1024]{2,1,0:T(1,128)S(1)} %reshape.63), channel_id=1, replica_groups=mesh['vocab'=64,'width'=8] {'vocab'}, dimensions={0}, use_global_device_ids=true | all-gather | bytes 266240 | tf_op jit(solution)/shard_map/all_gather | solution.py:11
  289.3 36.9 %all-gather.3 = f32[64,1,1024]{2,1,0:T(1,128)S(1)} all-gather(f32[1,1,1024]{2,1,0:T(1,128)S(1)} %reshape.65), channel_id=1, replica_groups=mesh['vocab'=64,'width'=8] {'vocab'}, dimensions={0}, use_global_device_ids=true | all-gather | bytes 266240 | tf_op jit(solution)/shard_map/all_gather | solution.py:11
  326.5 7.6 %while.33 = (s32[]{:T(128)}, f32[1024]{0:T(1024)S(1)}, f32[1024]{0:T(1024)S(1)}, f32[1024]{0:T(1024)S(1)}, f32[1024]{0:T(1024)S(1)}, /*index=5*/f32[63,1024]{1,0...) while((s32[]{:T(128)}, f32[1024]{0:T(1024)S(1)}, ...), condition=%wide.region_9.10_spmd, body=%wide.region_8.9_spmd.sunk | while | flops 16386 | bytes 110701 | solution.py:14
  334.1 0.6 subtract_multiply_fusion
  334.8 94.6 %psum.15 = f32[64]{0:T(128)S(1)} all-reduce(f32[64]{0:T(128)S(1)} %select_reduce_fusion.1), channel_id=1, replica_groups=mesh['vocab'=64,'width'=8] {'vocab','width'}, use_global_device_ids=true, to_apply=%region_12.13 | all-reduce | flops 64 | bytes 512 | tf_op jit(solution)/shard_map/psum | solution.py:95
  429.4 0.5 convert_divide_fusion
  (431 shorter events, 5.1 us)
Async XLA Ops:
  7.2 151.5 %all-gather.6.cloned.1.call-start = ((), (), s32[]{:S(2)}) async-start(), calls=%async_computation.2 | async-start | bytes 7372800 | tf_op jit(solution)/shard_map/all_gather | solution.py:61
  43.6 18.0 %copy-start.3 = (s32[16]{0:T(128)S(1)}, s32[16]{0:T(128)}, u32[]{:S(2)}) copy-start(s32[16]{0:T(128)} %param.13) | copy-start | bytes 196
  43.6 114.7 %copy-start.1 = (s32[64]{0:T(128)S(1)}, s32[64]{0:T(128)}, u32[]{:S(2)}) copy-start(s32[64]{0:T(128)} %param.15) | copy-start | bytes 772
  43.6 115.0 %all-to-all-start.1 = ((bf16[64,16,2048]{2,1,0:T(8,128)(2,1)}), bf16[64,16,2048]{2,1,0:T(8,128)(2,1)}, u32[]{:S(2)}, u32[]{:S(2)}) async-start(bf16[64,16,2048]{2,1,0:T(8,128)(2,1)} %stack.5), calls=%async_computation.1 | async-start | bytes 8388608 | tf_op jit(solution)/shard_map/all_to_all | solution.py:52
  174.8 159.3 %copy-start.2 = (s32[16]{0:T(128)S(1)}, s32[16]{0:T(128)}, u32[]{:S(2)}) copy-start(s32[16]{0:T(128)} %param.14) | copy-start | bytes 196
  334.7 95.2 %copy-start = (f32[16]{0:T(128)}, f32[16]{0:T(128)S(1)}, u32[]{:S(2)}) copy-start(f32[16]{0:T(128)S(1)} %get-tuple-element.158) | copy-start | bytes 196
Sparse Core Ops, SparseCore 0:
  10.0 90.4 all-gather.5
